TPU v7x, 32 devices: a whole 2x2x4 slice. The times are simulated.
32 devices in a mesh: tm: 8 (over z, core), space: 4 (over y, x).
Axes of the slice: x: 2, y: 2, z: 4, core: 2. Of those that a mesh axis runs over, the one named last changes fastest.
Arguments:
- snapshots: bfloat16 [4096, 1024], P('space', 'tm'), may hold values from -23 to 23
- energy: bfloat16 [32, 7, 128, 128], P('space'), may hold values from -0.375 to 0.375
- neighbours: int32 [32, 7], P('space'), may hold values from 0 to 31, as said below
- sketch: float32 [3, 256, 128], replicated, may hold values from -0.375 to 0.375
Outputs:
- modes: bfloat16 [4, 8, 4096, 128], P(None, 'tm', 'space')
Inputs may be any that keep to these rules, and one draw needn't show every extreme that they name: `neighbours`: entry [b, k] lies within 2 blocks of b.
All inputs are finite; a program needn't handle non-finite values.
Results may differ from a plain program's by a relative error of at most 0.017.
Values may be sent and summed in bfloat16 or wider, within the bound.
No kernel may reach another device: no remote copies, remote signals or barrier semaphores. Data moves between devices by JAX's collectives and lax.ppermute only.
A program may use at most 64 MiB of HBM per device.

v0:
```python
import jax
import jax.numpy as jnp
from jax import lax
from jax.sharding import PartitionSpec as P

HB = 2


def padded_2(cells, sides, width):
    for axis, dim in sides:
        count = lax.axis_size(axis)
        ends = count - 1
        head = lax.slice_in_dim(cells, 0, width, axis=dim)
        tail = lax.slice_in_dim(cells, cells.shape[dim] - width, cells.shape[dim], axis=dim)
        cells = jnp.concatenate(
            [
                lax.ppermute(tail, axis, [(i, (i + 1) % count) for i in range(ends)]),
                cells,
                lax.ppermute(head, axis, [((i + 1) % count, i) for i in range(ends)]),
            ],
            axis=dim,
        )
    return cells


def from_partner(value, axis, bit):
    mask = 2**bit
    pairs = [(source, source ^ mask) for source in range(lax.axis_size(axis))]
    return lax.ppermute(value, axis, pairs)


def blocked(matrix_rows, block_rows):
    return matrix_rows.reshape(matrix_rows.shape[0] // block_rows, block_rows, matrix_rows.shape[1])


def image_of(padded, source, energy, local_index):
    block_rows = energy.shape[2]
    running = 3.0 * blocked(source, block_rows).astype(jnp.float32)
    for slot_index in range(energy.shape[1]):
        gathered = jnp.take(padded, local_index[:, slot_index], axis=0)
        running = running + jnp.einsum(
            "nij,njw->niw", energy[:, slot_index], gathered, preferred_element_type=jnp.float32
        )
    return running.astype(jnp.bfloat16).reshape(source.shape[0], source.shape[1])


def gram_of(energy_image):
    return jnp.einsum("rc,rd->cd", energy_image, energy_image, preferred_element_type=jnp.float32)


def side_by_side(upper_half, first, second, axis_number):
    return jnp.where(
        upper_half,
        jnp.concatenate([second, first], axis_number),
        jnp.concatenate([first, second], axis_number),
    )


def on_device(snapshots, energy, neighbours, sketch):
    block_rows = energy.shape[2]
    block_count = energy.shape[0]
    rows_dev = snapshots.shape[0]
    total_rows = rows_dev * lax.axis_size("space")
    first_block = lax.axis_index("space") * block_count - HB
    local_index = neighbours - first_block
    window_index = lax.axis_index("tm")
    highest = lax.Precision.HIGHEST
    padded = padded_2(blocked(snapshots, block_rows), (("space", 0),), HB)
    energy_image = image_of(padded, snapshots, energy, local_index)
    gram_matrix = lax.psum(gram_of(energy_image), "space") / total_rows
    lower_factor = jnp.linalg.cholesky(gram_matrix)
    identity = jnp.eye(snapshots.shape[1], dtype=jnp.float32)
    coefficients = jax.scipy.linalg.solve_triangular(lower_factor, identity, lower=True).T.astype(
        jnp.bfloat16
    )
    current = jnp.dot(snapshots, coefficients, preferred_element_type=jnp.float32).astype(
        jnp.bfloat16
    )
    images = jnp.dot(energy_image, coefficients, preferred_element_type=jnp.float32).astype(
        jnp.bfloat16
    )
    levels_kept = [current]
    for tree_level in range(sketch.shape[0]):
        upper_half = window_index // 2**tree_level % 2 == 1
        partner, partner_image = from_partner((current, images), "tm", tree_level)
        joined = side_by_side(upper_half, current, partner, 1)
        joined_image = side_by_side(upper_half, images, partner_image, 1)
        sketch_level = sketch[tree_level]
        gram_matrix = lax.psum(gram_of(joined_image), "space") / total_rows
        columns = jnp.dot(gram_matrix, sketch_level, precision=highest)
        inner_gram = jnp.dot(
            columns.T, jnp.dot(gram_matrix, columns, precision=highest), precision=highest
        )
        lower_factor = jnp.linalg.cholesky(inner_gram)
        coefficients = jax.scipy.linalg.solve_triangular(
            lower_factor, columns.T, lower=True
        ).T.astype(jnp.bfloat16)
        new_modes = jnp.dot(joined, coefficients, preferred_element_type=jnp.float32).astype(
            jnp.bfloat16
        )
        new_image = jnp.dot(joined_image, coefficients, preferred_element_type=jnp.float32).astype(
            jnp.bfloat16
        )
        current = new_modes
        images = new_image
        levels_kept.append(current)
    return jnp.stack(levels_kept)[:, None]


def solution(mesh):
    placed = (P("space", "tm"), P("space", None, None, None), P("space", None), P())
    return jax.shard_map(
        on_device,
        mesh=mesh,
        in_specs=placed,
        out_specs=P(None, "tm", "space", None),
        check_vma=False,
    )
```

profile of v0, /device:TPU:0, one launch (start us, length us, event | category | flops | bytes accessed | tf_op | source)
XLA Modules:
  0.0 343.3 jit_solution(3305505052904443484)
XLA Ops:
  6.5 0.9 fusion.131
  7.4 1.3 collective-permute-start.1
  8.7 5.5 %collective-permute-start = (bf16[2,128,128]{2,1,0:T(8,128)(2,1)S(1)}, bf16[2,128,128]{2,1,0:T(8,128)(2,1)S(1)}, u32[]{:S(2)}, u32[]{:S(2)}) collective-permute-start(bf16[2,128,128]{2,1,0:T(8,128)(2,1)S(1)} %bitcast.162), channel_id=1, source_target_pairs={{0,1},{1,2},{2,3},{4,5},{5,6},{6,7},{8,9},{9,10},{10,11},{12,13},{... | collective-permute-start | bytes 196616 | tf_op jit(solution)/shard_map/ppermute | solution.py:17
  14.2 0.7 broadcast_subtract_fusion
  15.2 0.6 compare_and_fusion.6
  15.8 0.5 compare_and_fusion.2
  16.3 0.6 compare_and_fusion.4
  17.1 1.0 pad_maximum_fusion
  18.1 0.6 gather_fusion.6
  18.7 0.6 gather_fusion.5
  19.3 0.6 gather_fusion.4
  19.9 1.3 gather_fusion.3
  21.2 0.6 gather_fusion.2
  21.8 1.3 gather_fusion.1
  23.0 0.6 gather_fusion
  23.7 1.3 convolution_bitcast_fusion.5
  25.0 0.9 convolution_bitcast_fusion.4
  25.8 0.9 convolution_bitcast_fusion.3
  27.7 0.4 fusion.7
  28.1 0.9 convolution_bitcast_fusion.7
  29.1 44.5 %all-reduce.5.cloned.1.call-done = f32[128,128]{0,1:T(8,128)} async-done(((f32[128,128]{0,1:T(8,128)}), f32[128,128]{0,1:T(8,128)}) %all-reduce.5.cloned.1.call-update) | async-done | bytes 65552 | tf_op jit(solution)/shard_map/psum | solution.py:70
  73.6 0.8 broadcast_multiply_fusion
  74.5 0.9 fusion.109
  75.4 11.7 %cholesky.74 = f32[128,128]{1,0:T(8,128)S(1)} custom-call(f32[128,128]{1,0:T(8,128)S(1)} %fusion.109), custom_call_target="Cholesky" | custom-call | tf_op jit(solution)/shard_map/jit(cholesky)/cholesky | solution.py:71
  87.1 0.6 compare_reduce_fusion.3
  87.8 0.7 fusion.98
  88.4 9.8 %custom-call.9 = f32[1,128,128]{1,2,0:T(8,128)S(1)} custom-call(f32[1,128,128]{2,1,0:T(8,128)S(1)} %fusion.98), custom_call_target="InvertDiagBlocksLowerTriangular" | custom-call | tf_op jit(solution)/shard_map/jit(_solve_triangular)/triangular_solve | solution.py:73
  98.9 1.5 collective-permute-done.3
  100.4 1.1 fusion.97
  101.8 43.0 %all-reduce.7.cloned.1.call-done = f32[256,256]{1,0:T(8,128)} async-done(((f32[256,256]{1,0:T(8,128)}), f32[256,256]{1,0:T(8,128)}) %all-reduce.7.cloned.1.call-update) | async-done | bytes 262160 | tf_op jit(solution)/shard_map/psum | solution.py:89
  144.7 1.3 fusion.72
  146.1 1.3 fusion.70
  147.4 0.4 fusion.132
  147.9 11.7 %cholesky.85 = f32[128,128]{1,0:T(8,128)S(1)} custom-call(f32[128,128]{1,0:T(8,128)S(1)} %fusion.107), custom_call_target="Cholesky" | custom-call | tf_op jit(solution)/shard_map/jit(cholesky)/cholesky | solution.py:94
  159.6 0.6 compare_reduce_fusion.2
  160.3 0.7 fusion.99
  161.0 9.8 %custom-call.12 = f32[1,128,128]{1,2,0:T(8,128)S(1)} custom-call(f32[1,128,128]{2,1,0:T(8,128)S(1)} %fusion.99), custom_call_target="InvertDiagBlocksLowerTriangular" | custom-call | tf_op jit(solution)/shard_map/jit(_solve_triangular)/triangular_solve | solution.py:95
  170.8 0.3 convolution_convert_fusion.9
  171.4 1.6 collective-permute-start.5
  172.9 6.1 %collective-permute-done.5 = bf16[1024,128]{0,1:T(8,128)(2,1)S(1)} collective-permute-done((bf16[1024,128]{0,1:T(8,128)(2,1)S(1)}, bf16[1024,128]{0,1:T(8,128)(2,1)S(1)}, u32[]{:S(2)}, u32[]{:S(2)}) %collective-permute-start.5) | collective-permute-done | bytes 262176 | tf_op jit(solution)/shard_map/ppermute | solution.py:29
  179.0 1.1 fusion.96
  180.8 42.6 %all-reduce.9.cloned.1.call-done = f32[256,256]{1,0:T(8,128)} async-done(((f32[256,256]{1,0:T(8,128)}), f32[256,256]{1,0:T(8,128)}) %all-reduce.9.cloned.1.call-update) | async-done | bytes 262160 | tf_op jit(solution)/shard_map/psum | solution.py:89
  223.3 1.3 fusion.68
  224.7 1.3 fusion.66
  226.0 0.4 fusion.133
  226.5 11.7 %cholesky.96 = f32[128,128]{1,0:T(8,128)S(1)} custom-call(f32[128,128]{1,0:T(8,128)S(1)} %fusion.105), custom_call_target="Cholesky" | custom-call | tf_op jit(solution)/shard_map/jit(cholesky)/cholesky | solution.py:94
  238.2 0.6 compare_reduce_fusion.1
  238.9 0.7 fusion.100
  239.6 9.8 %custom-call.13 = f32[1,128,128]{1,2,0:T(8,128)S(1)} custom-call(f32[1,128,128]{2,1,0:T(8,128)S(1)} %fusion.100), custom_call_target="InvertDiagBlocksLowerTriangular" | custom-call | tf_op jit(solution)/shard_map/jit(_solve_triangular)/triangular_solve | solution.py:95
  250.0 2.5 collective-permute-start.7
  252.8 1.6 collective-permute-start.4
  254.3 9.9 %collective-permute-done.7 = bf16[1024,128]{0,1:T(8,128)(2,1)S(1)} collective-permute-done((bf16[1024,128]{0,1:T(8,128)(2,1)S(1)}, bf16[1024,128]{0,1:T(8,128)(2,1)S(1)}, u32[]{:S(2)}, u32[]{:S(2)}) %collective-permute-start.7) | collective-permute-done | bytes 262176 | tf_op jit(solution)/shard_map/ppermute | solution.py:29
  264.2 1.1 fusion.19
  265.7 0.3 collective-permute-start.6
  266.0 42.4 %all-reduce.11.cloned.1.call-done = f32[256,256]{1,0:T(8,128)} async-done(((f32[256,256]{1,0:T(8,128)}), f32[256,256]{1,0:T(8,128)}) %all-reduce.11.cloned.1.call-update) | async-done | bytes 262160 | tf_op jit(solution)/shard_map/psum | solution.py:89
  308.4 1.3 fusion.64
  309.8 1.3 fusion.62
  311.1 0.4 fusion.134
  311.6 12.0 %cholesky.107 = f32[128,128]{1,0:T(8,128)S(1)} custom-call(f32[128,128]{1,0:T(8,128)S(1)} %fusion.103), custom_call_target="Cholesky" | custom-call | tf_op jit(solution)/shard_map/jit(cholesky)/cholesky | solution.py:94
  323.6 0.6 compare_reduce_fusion
  324.3 0.7 fusion.101
  324.9 9.8 %custom-call.14 = f32[1,128,128]{1,2,0:T(8,128)S(1)} custom-call(f32[1,128,128]{2,1,0:T(8,128)S(1)} %fusion.101), custom_call_target="InvertDiagBlocksLowerTriangular" | custom-call | tf_op jit(solution)/shard_map/jit(_solve_triangular)/triangular_solve | solution.py:95
  334.7 0.3 convolution_convert_fusion.7
  335.5 1.3 copy.19
  (62 shorter events, 5.2 us)
Async XLA Ops:
  6.5 67.0 %all-reduce.5.cloned.1.call-start = ((), (), s32[]{:S(2)}) async-start(), calls=%async_computation | async-start | bytes 131072 | tf_op jit(solution)/shard_map/psum | solution.py:70
  7.4 9.6 %collective-permute-start.1 = (bf16[2,128,128]{2,1,0:T(8,128)(2,1)S(1)}, bf16[2,128,128]{2,1,0:T(8,128)(2,1)S(1)}, u32[]{:S(2)}, u32[]{:S(2)}) collective-permute-start(bf16[2,128,128]{2,1,0:T(8,128)(2,1)S(1)} %bitcast.163), channel_id=1, source_target_pairs={{1,0},{2,1},{3,2},{5,4},{6,5},{7,6},{9,8},{10,9},{11,10},{13,12},{... | collective-permute-start | bytes 196616 | tf_op jit(solution)/shard_map/ppermute | solution.py:19
  8.7 8.3 %collective-permute-start = (bf16[2,128,128]{2,1,0:T(8,128)(2,1)S(1)}, bf16[2,128,128]{2,1,0:T(8,128)(2,1)S(1)}, u32[]{:S(2)}, u32[]{:S(2)}) collective-permute-start(bf16[2,128,128]{2,1,0:T(8,128)(2,1)S(1)} %bitcast.162), channel_id=1, source_target_pairs={{0,1},{1,2},{2,3},{4,5},{5,6},{6,7},{8,9},{9,10},{10,11},{12,13},{... | collective-permute-start | bytes 196616 | tf_op jit(solution)/shard_map/ppermute | solution.py:17
  18.1 5.6 %copy-start.1 = (bf16[8,7,128,128]{3,2,1,0:T(8,128)(2,1)S(1)}, bf16[8,7,128,128]{3,2,1,0:T(8,128)(2,1)}, u32[]{:S(2)}) copy-start(bf16[8,7,128,128]{3,2,1,0:T(8,128)(2,1)} %param.10) | copy-start | bytes 5505028
  23.7 2.2 copy-start.2
  26.8 1.0 copy-start
  26.8 0.9 copy-start.4
  29.0 115.7 %all-reduce.7.cloned.1.call-start = ((), (), s32[]{:S(2)}) async-start(), calls=%async_computation.1 | async-start | bytes 524288 | tf_op jit(solution)/shard_map/psum | solution.py:89
  87.1 57.6 %copy-start.3 = (f32[3,256,128]{2,1,0:T(8,128)S(1)}, f32[3,256,128]{2,1,0:T(8,128)}, u32[]{:S(2)}) copy-start(f32[3,256,128]{2,1,0:T(8,128)} %param.12) | copy-start | bytes 1179652
  98.8 1.6 collective-permute-start.3
  101.5 121.8 %all-reduce.9.cloned.1.call-start = ((), (), s32[]{:S(2)}) async-start(), calls=%async_computation.2 | async-start | bytes 524288 | tf_op jit(solution)/shard_map/psum | solution.py:89
  171.4 7.6 %collective-permute-start.5 = (bf16[1024,128]{0,1:T(8,128)(2,1)S(1)}, bf16[1024,128]{0,1:T(8,128)(2,1)S(1)}, u32[]{:S(2)}, u32[]{:S(2)}) collective-permute-start(bf16[1024,128]{0,1:T(8,128)(2,1)S(1)} %convolution_convert_fusion.3), channel_id=1, source_target_pairs={{0,8},{4,12},{8,0},{12,4},{16,24},{20,28},{24,16},{28,20},{1,9},{5... | collective-permute-start | bytes 786440 | tf_op jit(solution)/shard_map/ppermute | solution.py:29
  180.2 128.3 %all-reduce.11.cloned.1.call-start = ((), (), s32[]{:S(2)}) async-start(), calls=%async_computation.3 | async-start | bytes 524288 | tf_op jit(solution)/shard_map/psum | solution.py:89
  180.7 71.8 %collective-permute-start.2 = (bf16[1024,128]{0,1:T(8,128)(2,1)S(1)}, bf16[1024,128]{0,1:T(8,128)(2,1)S(1)}, u32[]{:S(2)}, u32[]{:S(2)}) collective-permute-start(bf16[1024,128]{0,1:T(8,128)(2,1)S(1)} %bitcast.157), channel_id=1, source_target_pairs={{0,4},{4,0},{8,12},{12,8},{16,20},{20,16},{24,28},{28,24},{1,5},{5... | collective-permute-start | bytes 786440 | tf_op jit(solution)/shard_map/ppermute | solution.py:29
  250.0 14.3 %collective-permute-start.7 = (bf16[1024,128]{0,1:T(8,128)(2,1)S(1)}, bf16[1024,128]{0,1:T(8,128)(2,1)S(1)}, u32[]{:S(2)}, u32[]{:S(2)}) collective-permute-start(bf16[1024,128]{0,1:T(8,128)(2,1)S(1)} %convolution_convert_fusion.1), channel_id=1, source_target_pairs={{0,16},{4,20},{8,24},{12,28},{16,0},{20,4},{24,8},{28,12},{1,17},{... | collective-permute-start | bytes 786440 | tf_op jit(solution)/shard_map/ppermute | solution.py:29
  252.8 12.6 %collective-permute-start.4 = (bf16[1024,128]{0,1:T(8,128)(2,1)S(1)}, bf16[1024,128]{0,1:T(8,128)(2,1)S(1)}, u32[]{:S(2)}, u32[]{:S(2)}) collective-permute-start(bf16[1024,128]{0,1:T(8,128)(2,1)S(1)} %convolution_convert_fusion.4), channel_id=1, source_target_pairs={{0,8},{4,12},{8,0},{12,4},{16,24},{20,28},{24,16},{28,20},{1,9},{5... | collective-permute-start | bytes 786440 | tf_op jit(solution)/shard_map/ppermute | solution.py:29
  265.7 69.4 %collective-permute-start.6 = (bf16[1024,128]{0,1:T(8,128)(2,1)S(1)}, bf16[1024,128]{0,1:T(8,128)(2,1)S(1)}, u32[]{:S(2)}, u32[]{:S(2)}) collective-permute-start(bf16[1024,128]{0,1:T(8,128)(2,1)S(1)} %convolution_convert_fusion.2), channel_id=1, source_target_pairs={{0,16},{4,20},{8,24},{12,28},{16,0},{20,4},{24,8},{28,12},{1,17},{... | collective-permute-start | bytes 786440 | tf_op jit(solution)/shard_map/ppermute | solution.py:29
Sparse Core Ops, SparseCore 0:
  29.2 44.3 all-reduce.4
  101.7 43.0 all-reduce.6
  180.3 43.0 all-reduce.8
  265.5 42.9 all-reduce.10
where the time goes:
time: 344 us; the launch traced here: 343 us
  waiting for transfers between devices  190 us (55%)
  other arithmetic  97 us (28%)
  matrix products  20.8 us (6%)
  between operations  13.7 us (4%)
  starting transfers between devices  13.4 us (4%)
  local copies, waits for them, and re-layouts  8.4 us (2%)
    psum x3, waiting for transfers between devices, on_device(): gram_matrix = lax.psum(gram_of(joined_image), 'space') / total_rows  128 us
    psum x1, waiting for transfers between devices, on_device(): gram_matrix = lax.psum(gram_of(energy_image), 'space') / total_rows  44.5 us
    another operation x9, other arithmetic, on_device(): lower_factor = jnp.linalg.cholesky(inner_gram)  37.4 us
    another operation x6, other arithmetic, on_device(): jax.scipy.linalg.solve_triangular(lower_factor, columns.T, lower=True)  31.4 us
    ppermute x6, waiting for transfers between devices, from_partner(): return lax.ppermute(value, axis, pairs)  17.5 us
    another operation x3, other arithmetic, on_device(): lower_factor = jnp.linalg.cholesky(gram_matrix)  12.4 us
    another operation x2, other arithmetic, on_device(): jax.scipy.linalg.solve_triangular(lower_factor, identity, lower=True)  10.5 us
  transfers between devices with their start and end apart: 12, of which 7 were waited for; matrix products, arithmetic and copies ran while one was open for 17% of the time, Pallas kernels for 0%

commit v1 on v0

--- a/solution.py
+++ b/solution.py
@@ -4,6 +4,11 @@
 from jax.sharding import PartitionSpec as P
 
 HB = 2
+
+
+def summed_here(x, axis):
+    parts = lax.all_gather(x, axis)
+    return jnp.sum(parts, axis=0)
 
 
 def padded_2(cells, sides, width):
@@ -86,7 +91,7 @@
         joined = side_by_side(upper_half, current, partner, 1)
         joined_image = side_by_side(upper_half, images, partner_image, 1)
         sketch_level = sketch[tree_level]
-        gram_matrix = lax.psum(gram_of(joined_image), "space") / total_rows
+        gram_matrix = summed_here(gram_of(joined_image), "space") / total_rows
         columns = jnp.dot(gram_matrix, sketch_level, precision=highest)
         inner_gram = jnp.dot(
             columns.T, jnp.dot(gram_matrix, columns, precision=highest), precision=highest

time: 344 us -> 294 us (0.85)
  waiting for transfers between devices: 190 us -> 141 us
  matrix products: 20.8 us -> 14.9 us
    psum x3 -> x0, waiting for transfers between devices: 128 us -> none  [on_device(): gram_matrix = lax.psum(gram_of(joined_image), 'space') / total_rows]
    all_gather x0 -> x3, waiting for transfers between devices: none -> 66.4 us  [summed_here(): parts = lax.all_gather(x, axis)]
    ppermute x6, waiting for transfers between devices: 17.5 us -> 29.3 us  [from_partner(): return lax.ppermute(value, axis, pairs)]
    reduce_sum x0 -> x3, other arithmetic: none -> 3.96 us  [summed_here(): return jnp.sum(parts, axis=0)]
  transfers between devices with their start and end apart: 12 -> 12, of which waited for: 7 -> 9; matrix products, arithmetic and copies ran while one was open for 17% -> 10% of each run, Pallas kernels for 0% -> 0%
where the time goes in v1:
time: 294 us; the launch traced here: 293 us
  waiting for transfers between devices  141 us (48%)
  other arithmetic  100 us (34%)
  matrix products  14.9 us (5%)
  starting transfers between devices  14.2 us (5%)
  between operations  13.7 us (5%)
  local copies, waits for them, and re-layouts  9.08 us (3%)
    all_gather x3, waiting for transfers between devices, summed_here(): parts = lax.all_gather(x, axis)  66.4 us
    psum x1, waiting for transfers between devices, on_device(): gram_matrix = lax.psum(gram_of(energy_image), 'space') / total_rows  45 us
    another operation x9, other arithmetic, on_device(): lower_factor = jnp.linalg.cholesky(inner_gram)  37.4 us
    another operation x6, other arithmetic, on_device(): jax.scipy.linalg.solve_triangular(lower_factor, columns.T, lower=True)  31.4 us
    ppermute x6, waiting for transfers between devices, from_partner(): return lax.ppermute(value, axis, pairs)  29.3 us
    another operation x3, other arithmetic, on_device(): lower_factor = jnp.linalg.cholesky(gram_matrix)  12.4 us
    another operation x2, other arithmetic, on_device(): jax.scipy.linalg.solve_triangular(lower_factor, identity, lower=True)  10.5 us
    ppermute x6, starting transfers between devices, from_partner(): return lax.ppermute(value, axis, pairs)  6.91 us
  transfers between devices with their start and end apart: 12, of which 9 were waited for; matrix products, arithmetic and copies ran while one was open for 10% of the time, Pallas kernels for 0%

profile of v1, /device:TPU:0, one launch (start us, length us, event | category | flops | bytes accessed | tf_op | source)
XLA Modules:
  0.0 293.1 jit_solution(14254848844361291021)
XLA Ops:
  6.5 0.9 fusion.131
  7.4 1.3 collective-permute-start.1
  8.7 5.5 %collective-permute-start = (bf16[2,128,128]{2,1,0:T(8,128)(2,1)S(1)}, bf16[2,128,128]{2,1,0:T(8,128)(2,1)S(1)}, u32[]{:S(2)}, u32[]{:S(2)}) collective-permute-start(bf16[2,128,128]{2,1,0:T(8,128)(2,1)S(1)} %bitcast.168), channel_id=1, source_target_pairs={{0,1},{1,2},{2,3},{4,5},{5,6},{6,7},{8,9},{9,10},{10,11},{12,13},{... | collective-permute-start | bytes 196616 | tf_op jit(solution)/shard_map/ppermute | solution.py:22
  14.2 0.7 broadcast_subtract_fusion
  15.2 0.6 compare_and_fusion.6
  15.8 0.6 compare_and_fusion.4
  16.6 1.0 pad_maximum_fusion
  17.6 0.6 gather_fusion.6
  18.2 0.6 gather_fusion.5
  18.8 0.6 gather_fusion.4
  19.4 1.3 gather_fusion.3
  20.7 1.3 gather_fusion.2
  21.9 1.3 gather_fusion.1
  23.2 0.6 gather_fusion
  23.8 1.3 convolution_bitcast_fusion.5
  25.1 1.2 convolution_bitcast_fusion.4
  27.7 0.4 fusion.7
  28.0 0.9 convolution_bitcast_fusion.7
  29.0 45.0 %all-reduce.2.cloned.1.call-done = f32[128,128]{0,1:T(8,128)} async-done(((f32[128,128]{0,1:T(8,128)}), f32[128,128]{0,1:T(8,128)}) %all-reduce.2.cloned.1.call-update) | async-done | bytes 65552 | tf_op jit(solution)/shard_map/psum | solution.py:75
  74.0 0.8 broadcast_multiply_fusion
  75.0 0.9 fusion.109
  75.8 11.7 %cholesky.74 = f32[128,128]{1,0:T(8,128)S(1)} custom-call(f32[128,128]{1,0:T(8,128)S(1)} %fusion.109), custom_call_target="Cholesky" | custom-call | tf_op jit(solution)/shard_map/jit(cholesky)/cholesky | solution.py:76
  87.6 0.6 compare_reduce_fusion.3
  88.2 0.7 fusion.98
  88.9 9.8 %custom-call.9 = f32[1,128,128]{1,2,0:T(8,128)S(1)} custom-call(f32[1,128,128]{2,1,0:T(8,128)S(1)} %fusion.98), custom_call_target="InvertDiagBlocksLowerTriangular" | custom-call | tf_op jit(solution)/shard_map/jit(_solve_triangular)/triangular_solve | solution.py:78
  99.3 1.5 collective-permute-done.3
  100.8 1.1 fusion.97
  102.2 26.4 %all-gather.7.cloned.1.call-done = f32[1024,256]{1,0:T(8,128)} async-done(((f32[256,256]{1,0:T(8,128)}), f32[1024,256]{1,0:T(8,128)}) %all-gather.7.cloned.1.call-update) | async-done | bytes 1048592 | tf_op jit(solution)/shard_map/all_gather | solution.py:10
  128.6 1.3 reduce_sum.27
  129.9 0.4 fusion.72
  130.3 0.4 fusion.70
  130.7 0.4 fusion.132
  131.2 11.7 %cholesky.85 = f32[128,128]{1,0:T(8,128)S(1)} custom-call(f32[128,128]{1,0:T(8,128)S(1)} %fusion.107), custom_call_target="Cholesky" | custom-call | tf_op jit(solution)/shard_map/jit(cholesky)/cholesky | solution.py:99
  143.0 0.6 compare_reduce_fusion.2
  143.6 0.7 fusion.99
  144.3 9.8 %custom-call.12 = f32[1,128,128]{1,2,0:T(8,128)S(1)} custom-call(f32[1,128,128]{2,1,0:T(8,128)S(1)} %fusion.99), custom_call_target="InvertDiagBlocksLowerTriangular" | custom-call | tf_op jit(solution)/shard_map/jit(_solve_triangular)/triangular_solve | solution.py:100
  154.7 1.5 collective-permute-start.5
  156.2 6.4 %collective-permute-done.5 = bf16[1024,128]{0,1:T(8,128)(2,1)S(1)} collective-permute-done((bf16[1024,128]{0,1:T(8,128)(2,1)S(1)}, bf16[1024,128]{0,1:T(8,128)(2,1)S(1)}, u32[]{:S(2)}, u32[]{:S(2)}) %collective-permute-start.5) | collective-permute-done | bytes 262176 | tf_op jit(solution)/shard_map/ppermute | solution.py:34
  162.6 1.1 fusion.96
  164.1 26.4 %all-gather.9.cloned.1.call-done = f32[1024,256]{1,0:T(8,128)} async-done(((f32[256,256]{1,0:T(8,128)}), f32[1024,256]{1,0:T(8,128)}) %all-gather.9.cloned.1.call-update) | async-done | bytes 1048592 | tf_op jit(solution)/shard_map/all_gather | solution.py:10
  190.4 1.3 reduce_sum.28
  191.8 0.4 fusion.68
  192.1 0.4 fusion.66
  192.5 0.4 fusion.133
  193.0 11.7 %cholesky.96 = f32[128,128]{1,0:T(8,128)S(1)} custom-call(f32[128,128]{1,0:T(8,128)S(1)} %fusion.105), custom_call_target="Cholesky" | custom-call | tf_op jit(solution)/shard_map/jit(cholesky)/cholesky | solution.py:99
  204.8 0.6 compare_reduce_fusion.1
  205.4 0.7 fusion.100
  206.1 9.8 %custom-call.13 = f32[1,128,128]{1,2,0:T(8,128)S(1)} custom-call(f32[1,128,128]{2,1,0:T(8,128)S(1)} %fusion.100), custom_call_target="InvertDiagBlocksLowerTriangular" | custom-call | tf_op jit(solution)/shard_map/jit(_solve_triangular)/triangular_solve | solution.py:100
  216.5 2.5 collective-permute-start.7
  219.0 12.0 %collective-permute-done.7 = bf16[1024,128]{0,1:T(8,128)(2,1)S(1)} collective-permute-done((bf16[1024,128]{0,1:T(8,128)(2,1)S(1)}, bf16[1024,128]{0,1:T(8,128)(2,1)S(1)}, u32[]{:S(2)}, u32[]{:S(2)}) %collective-permute-start.7) | collective-permute-done | bytes 262176 | tf_op jit(solution)/shard_map/ppermute | solution.py:34
  231.0 1.1 fusion.19
  232.4 1.5 collective-permute-done.2
  234.3 0.6 collective-permute-start.4
  234.8 7.9 %collective-permute-done.4 = bf16[1024,128]{0,1:T(8,128)(2,1)S(1)} collective-permute-done((bf16[1024,128]{0,1:T(8,128)(2,1)S(1)}, bf16[1024,128]{0,1:T(8,128)(2,1)S(1)}, u32[]{:S(2)}, u32[]{:S(2)}) %collective-permute-start.4) | collective-permute-done | bytes 262176 | tf_op jit(solution)/shard_map/ppermute | solution.py:34
  243.0 2.2 collective-permute-start.6
  245.2 13.6 %all-gather.11.cloned.1.call-done = f32[1024,256]{1,0:T(8,128)} async-done(((f32[256,256]{1,0:T(8,128)}), f32[1024,256]{1,0:T(8,128)}) %all-gather.11.cloned.1.call-update) | async-done | bytes 1048592 | tf_op jit(solution)/shard_map/all_gather | solution.py:10
  258.8 1.3 reduce_sum.29
  260.1 0.4 fusion.64
  260.8 0.4 fusion.134
  261.3 11.9 %cholesky.107 = f32[128,128]{1,0:T(8,128)S(1)} custom-call(f32[128,128]{1,0:T(8,128)S(1)} %fusion.103), custom_call_target="Cholesky" | custom-call | tf_op jit(solution)/shard_map/jit(cholesky)/cholesky | solution.py:99
  273.3 0.6 compare_reduce_fusion
  274.0 0.7 fusion.101
  274.6 9.8 %custom-call.14 = f32[1,128,128]{1,2,0:T(8,128)S(1)} custom-call(f32[1,128,128]{2,1,0:T(8,128)S(1)} %fusion.101), custom_call_target="InvertDiagBlocksLowerTriangular" | custom-call | tf_op jit(solution)/shard_map/jit(_solve_triangular)/triangular_solve | solution.py:100
  285.2 1.3 copy.19
  (65 shorter events, 6.5 us)
Async XLA Ops:
  6.5 67.5 %all-reduce.2.cloned.1.call-start = ((), (), s32[]{:S(2)}) async-start(), calls=%async_computation | async-start | bytes 131072 | tf_op jit(solution)/shard_map/psum | solution.py:75
  7.4 9.1 %collective-permute-start.1 = (bf16[2,128,128]{2,1,0:T(8,128)(2,1)S(1)}, bf16[2,128,128]{2,1,0:T(8,128)(2,1)S(1)}, u32[]{:S(2)}, u32[]{:S(2)}) collective-permute-start(bf16[2,128,128]{2,1,0:T(8,128)(2,1)S(1)} %bitcast.169), channel_id=1, source_target_pairs={{1,0},{2,1},{3,2},{5,4},{6,5},{7,6},{9,8},{10,9},{11,10},{13,12},{... | collective-permute-start | bytes 196616 | tf_op jit(solution)/shard_map/ppermute | solution.py:24
  8.7 7.8 %collective-permute-start = (bf16[2,128,128]{2,1,0:T(8,128)(2,1)S(1)}, bf16[2,128,128]{2,1,0:T(8,128)(2,1)S(1)}, u32[]{:S(2)}, u32[]{:S(2)}) collective-permute-start(bf16[2,128,128]{2,1,0:T(8,128)(2,1)S(1)} %bitcast.168), channel_id=1, source_target_pairs={{0,1},{1,2},{2,3},{4,5},{5,6},{6,7},{8,9},{9,10},{10,11},{12,13},{... | collective-permute-start | bytes 196616 | tf_op jit(solution)/shard_map/ppermute | solution.py:22
  17.6 6.3 %copy-start.1 = (bf16[8,7,128,128]{3,2,1,0:T(8,128)(2,1)S(1)}, bf16[8,7,128,128]{3,2,1,0:T(8,128)(2,1)}, u32[]{:S(2)}) copy-start(bf16[8,7,128,128]{3,2,1,0:T(8,128)(2,1)} %param.10) | copy-start | bytes 5505028
  23.8 2.6 copy-start.2
  26.7 1.0 copy-start
  26.7 0.9 copy-start.4
  29.0 99.6 %all-gather.7.cloned.1.call-start = ((), (), s32[]{:S(2)}) async-start(), calls=%async_computation.1 | async-start | bytes 1310720 | tf_op jit(solution)/shard_map/all_gather | solution.py:10
  99.2 1.6 collective-permute-start.3
  99.3 30.6 %copy-start.3 = (f32[3,256,128]{2,1,0:T(8,128)S(1)}, f32[3,256,128]{2,1,0:T(8,128)}, u32[]{:S(2)}) copy-start(f32[3,256,128]{2,1,0:T(8,128)} %param.12) | copy-start | bytes 1179652
  102.0 88.5 %all-gather.9.cloned.1.call-start = ((), (), s32[]{:S(2)}) async-start(), calls=%async_computation.2 | async-start | bytes 1310720 | tf_op jit(solution)/shard_map/all_gather | solution.py:10
  154.7 7.9 %collective-permute-start.5 = (bf16[1024,128]{0,1:T(8,128)(2,1)S(1)}, bf16[1024,128]{0,1:T(8,128)(2,1)S(1)}, u32[]{:S(2)}, u32[]{:S(2)}) collective-permute-start(bf16[1024,128]{0,1:T(8,128)(2,1)S(1)} %convolution_convert_fusion.3), channel_id=1, source_target_pairs={{0,8},{4,12},{8,0},{12,4},{16,24},{20,28},{24,16},{28,20},{1,9},{5... | collective-permute-start | bytes 786440 | tf_op jit(solution)/shard_map/ppermute | solution.py:34
  163.8 95.0 %all-gather.11.cloned.1.call-start = ((), (), s32[]{:S(2)}) async-start(), calls=%async_computation.3 | async-start | bytes 1310720 | tf_op jit(solution)/shard_map/all_gather | solution.py:10
  216.5 14.4 %collective-permute-start.7 = (bf16[1024,128]{0,1:T(8,128)(2,1)S(1)}, bf16[1024,128]{0,1:T(8,128)(2,1)S(1)}, u32[]{:S(2)}, u32[]{:S(2)}) collective-permute-start(bf16[1024,128]{0,1:T(8,128)(2,1)S(1)} %convolution_convert_fusion.1), channel_id=1, source_target_pairs={{0,16},{4,20},{8,24},{12,28},{16,0},{20,4},{24,8},{28,12},{1,17},{... | collective-permute-start | bytes 786440 | tf_op jit(solution)/shard_map/ppermute | solution.py:34
  232.4 1.6 collective-permute-start.2
  234.3 8.4 %collective-permute-start.4 = (bf16[1024,128]{0,1:T(8,128)(2,1)S(1)}, bf16[1024,128]{0,1:T(8,128)(2,1)S(1)}, u32[]{:S(2)}, u32[]{:S(2)}) collective-permute-start(bf16[1024,128]{0,1:T(8,128)(2,1)S(1)} %convolution_convert_fusion.4), channel_id=1, source_target_pairs={{0,8},{4,12},{8,0},{12,4},{16,24},{20,28},{24,16},{28,20},{1,9},{5... | collective-permute-start | bytes 786440 | tf_op jit(solution)/shard_map/ppermute | solution.py:34
  243.0 41.8 %collective-permute-start.6 = (bf16[1024,128]{0,1:T(8,128)(2,1)S(1)}, bf16[1024,128]{0,1:T(8,128)(2,1)S(1)}, u32[]{:S(2)}, u32[]{:S(2)}) collective-permute-start(bf16[1024,128]{0,1:T(8,128)(2,1)S(1)} %convolution_convert_fusion.2), channel_id=1, source_target_pairs={{0,16},{4,20},{8,24},{12,28},{16,0},{20,4},{24,8},{28,12},{1,17},{... | collective-permute-start | bytes 786440 | tf_op jit(solution)/shard_map/ppermute | solution.py:34
Sparse Core Ops, SparseCore 0:
  29.1 44.8 all-reduce.1
  102.1 26.4 all-gather.6
  163.9 26.4 all-gather.8
  232.2 26.4 all-gather.10
